TPU v7x, 512 devices: a whole 4x8x8 slice. The times are simulated.
512 devices in a mesh: row: 16 (over y, core), col: 32 (over x, z).
Axes of the slice: x: 4, y: 8, z: 8, core: 2. Of those that a mesh axis runs over, the one named last changes fastest.
Arguments:
- positions: float32 [4, 4096, 4096], P(None, 'row', 'col'), may hold values from -2 to 2, as said below
Outputs:
- rotated: float32 [4, 4096, 4096], P(None, 'row', 'col')
Inputs may be any that keep to these rules, and one draw needn't show every extreme that they name: `positions`: each of the 4 matrices is symmetric.
All inputs are finite; a program needn't handle non-finite values.
Results may differ from a plain program's by a relative error of at most 0.00026.
Values sent between devices are 32-bit elements; how exact they have to be, the bound alone decides.
A program may use at most 64 MiB of HBM per device.

v0:
```python
import jax
import jax.numpy as jnp
from jax import lax
from jax.sharding import PartitionSpec as P

TERMS = 4


STEP_SIZE = 0.4
HIGHEST = lax.Precision.HIGHEST


def partner_2(value, axis, bit):
    mask = 2**bit
    pairs = [(source, source ^ mask) for source in range(lax.axis_size(axis))]
    return lax.ppermute(value, axis, pairs)


def broadcast(array, axis, root):
    return lax.dynamic_index_in_dim(lax.all_gather(array, axis), root, 0, keepdims=False)


def regroup(tile_set):
    half_rows = tile_set.shape[1] // 2
    is_upper = lax.axis_index("row") >= lax.axis_size("row") // 2
    outgoing = jnp.where(is_upper, tile_set[:, :half_rows], tile_set[:, half_rows:])
    arrived = partner_2(outgoing, "row", lax.axis_size("row").bit_length() - 2)
    upper_result = jnp.concatenate((arrived, tile_set[:, half_rows:]), axis=1)
    lower_result = jnp.concatenate((tile_set[:, :half_rows], arrived), axis=1)
    return jnp.where(is_upper, upper_result, lower_result)


def taylor_columns(generator, start_columns):
    current = start_columns
    summed = start_columns
    for power in range(1, TERMS + 1):
        current = (
            jnp.dot(generator, current, precision=HIGHEST, preferred_element_type=jnp.float32)
            / power
        )
        summed = summed + current
    return summed


def times_weights(tile_set, weights):
    return jnp.einsum("kai,ib->kab", tile_set, weights, precision=HIGHEST)


def jacobi_round(tile_set, late):
    block_width = tile_set.shape[2]
    pair_rows = tile_set.shape[1]
    row_count = lax.axis_size("row")
    col_count = lax.axis_size("col")
    row_id = lax.axis_index("row")
    col_id = lax.axis_index("col")
    if late:
        stride = col_count // 2
        column_bit = col_count.bit_length() - 2
        first_block = 2 * row_id - jnp.where(row_id >= row_count // 2, stride - 1, 0)
        column_root = col_id % stride // 2 + col_id % 2 * (row_count // 2)
        col_first = col_id < stride
    else:
        stride = 1
        column_bit = 0
        first_block = 2 * row_id
        column_root = col_id // 2
        col_first = col_id % 2 == 0
    second_block = first_block + stride
    on_diagonal = jnp.logical_or(col_id == first_block, col_id == second_block)
    offset = jnp.where(col_first, 0, block_width)
    other_offset = block_width - offset
    own_rows = lax.dynamic_slice_in_dim(tile_set, offset, block_width, 1)
    own_centres = jnp.diagonal(own_rows, axis1=1, axis2=2)
    other_centres = partner_2(own_centres, "col", column_bit)
    pair_centres = jnp.where(
        col_first,
        jnp.concatenate((own_centres, other_centres), axis=1),
        jnp.concatenate((other_centres, own_centres), axis=1),
    )
    half_generator = jnp.sum(
        tile_set * (own_centres[:, None, :] - pair_centres[:, :, None]), axis=0
    )
    other_generator = partner_2(half_generator, "col", column_bit)
    generator = STEP_SIZE * jnp.where(
        col_first,
        jnp.concatenate((half_generator, other_generator), axis=1),
        jnp.concatenate((other_generator, half_generator), axis=1),
    )
    identity = jnp.eye(pair_rows, dtype=jnp.float32)
    start_columns = lax.dynamic_slice_in_dim(identity, offset, block_width, 1)
    own_rotation = lax.cond(
        on_diagonal,
        lambda: taylor_columns(generator, start_columns),
        lambda: jnp.zeros_like(start_columns),
    )
    left_columns = broadcast(own_rotation, "col", first_block)
    right_columns = broadcast(own_rotation, "col", second_block)
    full_rotation = jnp.concatenate((left_columns, right_columns), axis=1)
    column_rotation = broadcast(own_rotation, "row", column_root)
    own_weights = lax.dynamic_slice_in_dim(column_rotation, offset, block_width, 0)
    other_weights = lax.dynamic_slice_in_dim(column_rotation, other_offset, block_width, 0)
    partner = partner_2(tile_set, "col", column_bit)
    right_side = times_weights(tile_set, own_weights) + times_weights(partner, other_weights)
    return jnp.einsum("ia,kib->kab", full_rotation, right_side, precision=HIGHEST)


def local(positions):
    tile_set = jacobi_round(positions, False)
    tile_set = regroup(tile_set)
    tile_set = jacobi_round(tile_set, True)
    return regroup(tile_set)


def solution(mesh):
    placed = (P(None, "row", "col"),)
    return jax.shard_map(
        local, mesh=mesh, in_specs=placed, out_specs=P(None, "row", "col"), check_vma=False
    )
```

profile of v0, /device:TPU:16, one launch (start us, length us, event | category | flops | bytes accessed | tf_op | source)
XLA Modules:
  0.0 363.9 jit_solution(14608897538515197148)
XLA Ops:
  7.5 4.7 %copy.24 = f32[4,128,128]{0,2,1:T(8,128)} copy(f32[4,128,128]{2,1,0:T(8,128)S(1)} %constant_dynamic-slice_fusion.1) | data formatting | bytes 524288
  12.2 1.8 gather_fusion
  14.0 4.3 %collective-permute-start = (f32[4,128]{0,1:T(8,128)S(1)}, f32[4,128]{0,1:T(8,128)S(1)}, u32[]{:S(2)}, u32[]{:S(2)}) collective-permute-start(f32[4,128]{0,1:T(8,128)S(1)} %bitcast.66), channel_id=1, source_target_pairs={{0,1},{1,0},{2,3},{3,2},{4,5},{5,4},{6,7},{7,6},{8,9},{9,8},{10,11... | collective-permute-start | bytes 6152 | tf_op jit(solution)/shard_map/ppermute | solution.py:16
  18.3 2.2 collective-permute-done
  20.8 3.9 %collective-permute-start.1 = (f32[256,128]{1,0:T(8,128)S(1)}, f32[256,128]{1,0:T(8,128)S(1)}, u32[]{:S(2)}, u32[]{:S(2)}) collective-permute-start(f32[256,128]{1,0:T(8,128)S(1)} %multiply_reduce_fusion.1), channel_id=1, source_target_pairs={{0,1},{1,0},{2,3},{3,2},{4,5},{5,4},{6,7},{7,6},{8,9},{9,8},{10,11... | collective-permute-start | bytes 393224 | tf_op jit(solution)/shard_map/ppermute | solution.py:16
  24.8 2.9 collective-permute-done.1
  29.3 3.9 %collective-permute-start.2 = (f32[4,256,128]{2,1,0:T(8,128)S(1)}, f32[4,256,128]{2,1,0:T(8,128)S(1)}, u32[]{:S(2)}, u32[]{:S(2)}) collective-permute-start(f32[4,256,128]{2,1,0:T(8,128)S(1)} %copy-done), channel_id=1, source_target_pairs={{0,1},{1,0},{2,3},{3,2},{4,5},{5,4},{6,7},{7,6},{8,9},{9,8},{10,11... | collective-permute-start | bytes 1572872 | tf_op jit(solution)/shard_map/ppermute | solution.py:16
  33.2 40.8 %all-gather.5.cloned.1.call-done = f32[16,256,128]{2,1,0:T(8,128)} async-done(((f32[1,256,128]{2,1,0:T(8,128)}), f32[16,256,128]{2,1,0:T(8,128)}) %all-gather.5.cloned.1.call-update) | async-done | bytes 2097168 | tf_op jit(solution)/shard_map/all_gather | solution.py:20
  74.1 1.5 fusion.20
  77.2 88.4 %all-gather.7.cloned.1.call-done = f32[32,256,128]{2,1,0:T(8,128)} async-done(((f32[1,256,128]{2,1,0:T(8,128)}), f32[32,256,128]{2,1,0:T(8,128)}) %all-gather.7.cloned.1.call-update) | async-done | bytes 4194320 | tf_op jit(solution)/shard_map/all_gather | solution.py:20
  167.2 5.6 %collective-permute-start.3 = (f32[4,128,128]{1,2,0:T(8,128)S(1)}, f32[4,128,128]{1,2,0:T(8,128)S(1)}, u32[]{:S(2)}, u32[]{:S(2)}) collective-permute-start(f32[4,128,128]{1,2,0:T(8,128)S(1)} %get-tuple-element.97), channel_id=1, source_target_pairs={{0,256},{32,288},{64,320},{96,352},{128,384},{160,416},{192,448},{... | collective-permute-start | bytes 786440 | tf_op jit(solution)/shard_map/ppermute | solution.py:16
  172.8 10.1 %collective-permute-done.3 = f32[4,128,128]{1,2,0:T(8,128)S(1)} collective-permute-done((f32[4,128,128]{1,2,0:T(8,128)S(1)}, f32[4,128,128]{1,2,0:T(8,128)S(1)}, u32[]{:S(2)}, u32[]{:S(2)}) %collective-permute-start.3) | collective-permute-done | bytes 262176 | tf_op jit(solution)/shard_map/ppermute | solution.py:16
  183.0 7.6 %copy.15 = f32[4,128,128]{0,2,1:T(8,128)} copy(f32[4,128,128]{1,2,0:T(8,128)S(1)} %constant_dynamic-slice_fusion) | data formatting | bytes 524288 | tf_op jit(solution)/shard_map/dynamic_slice | solution.py:72
  190.6 1.8 gather_fusion.1
  192.4 3.4 collective-permute-start.4
  195.8 4.2 %collective-permute-done.4 = f32[4,128]{0,1:T(8,128)S(1)} collective-permute-done((f32[4,128]{0,1:T(8,128)S(1)}, f32[4,128]{0,1:T(8,128)S(1)}, u32[]{:S(2)}, u32[]{:S(2)}) %collective-permute-start.4) | collective-permute-done | bytes 2080 | tf_op jit(solution)/shard_map/ppermute | solution.py:16
  200.3 3.4 collective-permute-start.5
  203.7 5.0 %collective-permute-done.5 = f32[256,128]{0,1:T(8,128)S(1)} collective-permute-done((f32[256,128]{0,1:T(8,128)S(1)}, f32[256,128]{0,1:T(8,128)S(1)}, u32[]{:S(2)}, u32[]{:S(2)}) %collective-permute-start.5) | collective-permute-done | bytes 131104 | tf_op jit(solution)/shard_map/ppermute | solution.py:16
  210.0 3.4 collective-permute-start.6
  213.4 9.6 %collective-permute-done.6 = f32[4,256,128]{1,2,0:T(8,128)S(1)} collective-permute-done((f32[4,256,128]{1,2,0:T(8,128)S(1)}, f32[4,256,128]{1,2,0:T(8,128)S(1)}, u32[]{:S(2)}, u32[]{:S(2)}) %collective-permute-start.6) | collective-permute-done | bytes 524320 | tf_op jit(solution)/shard_map/ppermute | solution.py:16
  223.0 24.6 %all-gather.9.cloned.1.call-done = f32[16,256,128]{2,1,0:T(8,128)} async-done(((f32[1,256,128]{2,1,0:T(8,128)}), f32[16,256,128]{2,1,0:T(8,128)}) %all-gather.9.cloned.1.call-update) | async-done | bytes 2097168 | tf_op jit(solution)/shard_map/all_gather | solution.py:20
  250.6 88.3 %all-gather.11.cloned.1.call-done = f32[32,256,128]{2,1,0:T(8,128)} async-done(((f32[1,256,128]{2,1,0:T(8,128)}), f32[32,256,128]{2,1,0:T(8,128)}) %all-gather.11.cloned.1.call-update) | async-done | bytes 4194320 | tf_op jit(solution)/shard_map/all_gather | solution.py:20
  340.6 5.6 %collective-permute-start.7 = (f32[4,128,128]{1,2,0:T(8,128)S(1)}, f32[4,128,128]{1,2,0:T(8,128)S(1)}, u32[]{:S(2)}, u32[]{:S(2)}) collective-permute-start(f32[4,128,128]{1,2,0:T(8,128)S(1)} %get-tuple-element.94), channel_id=1, source_target_pairs={{0,256},{32,288},{64,320},{96,352},{128,384},{160,416},{192,448},{... | collective-permute-start | bytes 786440 | tf_op jit(solution)/shard_map/ppermute | solution.py:16
  346.1 10.2 %collective-permute-done.7 = f32[4,128,128]{1,2,0:T(8,128)S(1)} collective-permute-done((f32[4,128,128]{1,2,0:T(8,128)S(1)}, f32[4,128,128]{1,2,0:T(8,128)S(1)}, u32[]{:S(2)}, u32[]{:S(2)}) %collective-permute-start.7) | collective-permute-done | bytes 262176 | tf_op jit(solution)/shard_map/ppermute | solution.py:16
  (46 shorter events, 13.4 us)
Async XLA Ops:
  6.5 67.5 %all-gather.5.cloned.1.call-start = ((), (), s32[]{:S(2)}) async-start(), calls=%async_computation | async-start | bytes 2228224 | tf_op jit(solution)/shard_map/all_gather | solution.py:20
  7.5 13.1 %copy-start = (f32[4,256,128]{2,1,0:T(8,128)S(1)}, f32[4,256,128]{2,1,0:T(8,128)}, u32[]{:S(2)}) copy-start(f32[4,256,128]{2,1,0:T(8,128)} %param.5) | copy-start | bytes 1572868
  14.0 6.5 %collective-permute-start = (f32[4,128]{0,1:T(8,128)S(1)}, f32[4,128]{0,1:T(8,128)S(1)}, u32[]{:S(2)}, u32[]{:S(2)}) collective-permute-start(f32[4,128]{0,1:T(8,128)S(1)} %bitcast.66), channel_id=1, source_target_pairs={{0,1},{1,0},{2,3},{3,2},{4,5},{5,4},{6,7},{7,6},{8,9},{9,8},{10,11... | collective-permute-start | bytes 6152 | tf_op jit(solution)/shard_map/ppermute | solution.py:16
  20.8 6.9 %collective-permute-start.1 = (f32[256,128]{1,0:T(8,128)S(1)}, f32[256,128]{1,0:T(8,128)S(1)}, u32[]{:S(2)}, u32[]{:S(2)}) collective-permute-start(f32[256,128]{1,0:T(8,128)S(1)} %multiply_reduce_fusion.1), channel_id=1, source_target_pairs={{0,1},{1,0},{2,3},{3,2},{4,5},{5,4},{6,7},{7,6},{8,9},{9,8},{10,11... | collective-permute-start | bytes 393224 | tf_op jit(solution)/shard_map/ppermute | solution.py:16
  27.8 0.7 copy-start.1
  28.5 137.1 %all-gather.7.cloned.1.call-start = ((), (), s32[]{:S(2)}) async-start(), calls=%async_computation.1 | async-start | bytes 4325376 | tf_op jit(solution)/shard_map/all_gather | solution.py:20
  29.2 218.4 %all-gather.9.cloned.1.call-start = ((), (), s32[]{:S(2)}) async-start(), calls=%async_computation.2 | async-start | bytes 2228224 | tf_op jit(solution)/shard_map/all_gather | solution.py:20
  29.3 46.4 %collective-permute-start.2 = (f32[4,256,128]{2,1,0:T(8,128)S(1)}, f32[4,256,128]{2,1,0:T(8,128)S(1)}, u32[]{:S(2)}, u32[]{:S(2)}) collective-permute-start(f32[4,256,128]{2,1,0:T(8,128)S(1)} %copy-done), channel_id=1, source_target_pairs={{0,1},{1,0},{2,3},{3,2},{4,5},{5,4},{6,7},{7,6},{8,9},{9,8},{10,11... | collective-permute-start | bytes 1572872 | tf_op jit(solution)/shard_map/ppermute | solution.py:16
  167.2 15.7 %collective-permute-start.3 = (f32[4,128,128]{1,2,0:T(8,128)S(1)}, f32[4,128,128]{1,2,0:T(8,128)S(1)}, u32[]{:S(2)}, u32[]{:S(2)}) collective-permute-start(f32[4,128,128]{1,2,0:T(8,128)S(1)} %get-tuple-element.97), channel_id=1, source_target_pairs={{0,256},{32,288},{64,320},{96,352},{128,384},{160,416},{192,448},{... | collective-permute-start | bytes 786440 | tf_op jit(solution)/shard_map/ppermute | solution.py:16
  192.4 7.7 %collective-permute-start.4 = (f32[4,128]{0,1:T(8,128)S(1)}, f32[4,128]{0,1:T(8,128)S(1)}, u32[]{:S(2)}, u32[]{:S(2)}) collective-permute-start(f32[4,128]{0,1:T(8,128)S(1)} %bitcast.64), channel_id=1, source_target_pairs={{0,16},{1,17},{2,18},{3,19},{4,20},{5,21},{6,22},{7,23},{8,24},{9,... | collective-permute-start | bytes 6152 | tf_op jit(solution)/shard_map/ppermute | solution.py:16
  200.3 8.4 %collective-permute-start.5 = (f32[256,128]{0,1:T(8,128)S(1)}, f32[256,128]{0,1:T(8,128)S(1)}, u32[]{:S(2)}, u32[]{:S(2)}) collective-permute-start(f32[256,128]{0,1:T(8,128)S(1)} %multiply_reduce_fusion), channel_id=1, source_target_pairs={{0,16},{1,17},{2,18},{3,19},{4,20},{5,21},{6,22},{7,23},{8,24},{9,... | collective-permute-start | bytes 393224 | tf_op jit(solution)/shard_map/ppermute | solution.py:16
  208.8 0.7 copy-start.2
  209.4 129.5 %all-gather.11.cloned.1.call-start = ((), (), s32[]{:S(2)}) async-start(), calls=%async_computation.3 | async-start | bytes 4325376 | tf_op jit(solution)/shard_map/all_gather | solution.py:20
  210.0 13.0 %collective-permute-start.6 = (f32[4,256,128]{1,2,0:T(8,128)S(1)}, f32[4,256,128]{1,2,0:T(8,128)S(1)}, u32[]{:S(2)}, u32[]{:S(2)}) collective-permute-start(f32[4,256,128]{1,2,0:T(8,128)S(1)} %maximum_select_fusion), channel_id=1, source_target_pairs={{0,16},{1,17},{2,18},{3,19},{4,20},{5,21},{6,22},{7,23},{8,24},{9,... | collective-permute-start | bytes 1572872 | tf_op jit(solution)/shard_map/ppermute | solution.py:16
  340.6 15.7 %collective-permute-start.7 = (f32[4,128,128]{1,2,0:T(8,128)S(1)}, f32[4,128,128]{1,2,0:T(8,128)S(1)}, u32[]{:S(2)}, u32[]{:S(2)}) collective-permute-start(f32[4,128,128]{1,2,0:T(8,128)S(1)} %get-tuple-element.94), channel_id=1, source_target_pairs={{0,256},{32,288},{64,320},{96,352},{128,384},{160,416},{192,448},{... | collective-permute-start | bytes 786440 | tf_op jit(solution)/shard_map/ppermute | solution.py:16
Sparse Core Ops, SparseCore 0:
  28.6 45.4 all-gather.4
  77.2 88.2 all-gather.6
  209.6 38.0 all-gather.8
  250.6 88.2 all-gather.10
where the time goes:
time: 364 us
  waiting for transfers between devices  288 us (79%)
  starting transfers between devices  33.5 us (9%)
  local copies, waits for them, and re-layouts  21.4 us (6%)
  between operations  13.5 us (4%)
  matrix products  7.2 us (2%)
    all_gather x4, waiting for transfers between devices, broadcast(): lax.all_gather(array, axis)  242 us
    ppermute x8, waiting for transfers between devices, partner_2(): return lax.ppermute(value, axis, pairs)  44.1 us
    ppermute x8, starting transfers between devices, partner_2(): return lax.ppermute(value, axis, pairs)  33.3 us
    dynamic_slice x3, local copies, waits for them, and re-layouts, jacobi_round(): own_rows = lax.dynamic_slice_in_dim(tile_set, offset, block_width, 1)  8.64 us
  transfers between devices with their start and end apart: 12, of which 11 were waited for; matrix products, arithmetic and copies ran while one was open for 2% of the time, Pallas kernels for 0%

commit v1 on v0

v1 whole, which is shorter than its diff:
```python
import functools

import jax
import jax.numpy as jnp
from jax import lax
from jax.experimental import pallas as pl
from jax.experimental.pallas import tpu as pltpu
from jax.sharding import PartitionSpec as P

STEP_SIZE = 0.4
B = 128
MESH = pl.DeviceIdType.MESH
F32 = jnp.float32
BF16 = jnp.bfloat16
REACH = {1: (0,), 2: (0, 1), 4: (2, 1, -1, 0)}


def split(value):
    high = value.astype(BF16)
    return high, (value - high.astype(F32)).astype(BF16)


def product(left, right):
    dot = functools.partial(jnp.dot, preferred_element_type=F32)
    return dot(left[0], right[0]) + (dot(left[0], right[1]) + dot(left[1], right[0]))


def block(index):
    return pl.ds(index * B, B)


def kernel(
    n_row,
    n_col,
    pos_ref,
    out_ref,
    quad,
    half_done,
    turned,
    parts,
    arrived,
    gen,
    full,
    rows_high,
    rows_low,
    cols_high,
    cols_low,
    done,
    landed,
    keep_sem,
    p_send,
    p_recv,
    y_send,
    y_recv,
    r_send,
    r_recv,
    a_send,
    a_recv,
    b_send,
    b_recv,
    z_send,
    z_recv,
):
    n_quad = n_col // 4
    row = lax.axis_index("row")
    col = lax.axis_index("col")
    row_quad, upper = lax.rem(row, n_quad), lax.div(row, n_quad)
    col_high, low = lax.div(col, n_col // 2), lax.rem(col, 2)
    col_quad = lax.div(lax.rem(col, n_col // 2), 2)
    mine = 2 * col_high + low
    on_diagonal = row_quad == col_quad
    off_diagonal = row_quad != col_quad
    far_row = lax.rem(row + n_quad, n_row)

    def column(quad_id, place):
        return (n_col // 2) * lax.div(place, 2) + 2 * quad_id + lax.rem(place, 2)

    def peer(step):
        place = lax.rem(mine + step, 4)
        return place, (row, column(col_quad, place))

    def sender(step):
        return lax.rem(mine + 4 - step, 4)

    def remote(src, dst, send, recv, device):
        return pltpu.make_async_remote_copy(
            src_ref=src, dst_ref=dst, send_sem=send, recv_sem=recv, device_id=device, device_id_type=MESH
        )

    reach = REACH[n_row // 4]
    row_targets = [(row, column(lax.rem(row_quad + hop, n_quad), mine)) for hop in range(1, n_quad)]
    chip, core = lax.div(row, 2), lax.rem(row, 2)
    col_targets = []
    for hop in reach:
        there = lax.rem(chip + n_row // 2 + hop, n_row // 2)
        col_targets.append((2 * there + 1 - core, col))
        if hop != 0:
            col_targets.append((2 * there + core, col))
    row_source = (row, column(row_quad, mine))
    away = lax.rem(chip + n_row // 2 - lax.div(col_quad, 2), n_row // 2)
    wraps = lax.div(away + n_row // 8 - (1 if n_row >= 16 else 0), n_row // 4) if n_row >= 16 else lax.div(away, n_row // 4)
    col_source = (lax.rem(col_quad + n_quad * lax.rem(wraps, 2), n_row), col)

    barrier = pltpu.get_barrier_semaphore()
    for step in (1, 2, 3):
        pl.semaphore_signal(barrier, inc=1, device_id=(row, column(col_quad, sender(step))), device_id_type=MESH)
    pl.semaphore_signal(barrier, inc=1, device_id=(far_row, col), device_id_type=MESH)

    @pl.when(off_diagonal)
    def _():
        pl.semaphore_signal(barrier, inc=1, device_id=row_source, device_id_type=MESH)
        pl.semaphore_signal(barrier, inc=1, device_id=col_source, device_id_type=MESH)
        pl.semaphore_wait(barrier, 4)

    @pl.when(on_diagonal)
    def _():
        pl.semaphore_wait(barrier, 4 + len(row_targets) + len(col_targets))

    own_rows = pl.ds(pl.multiple_of(upper * 2 * B, 2 * B), 2 * B)
    far_rows = pl.ds(pl.multiple_of((1 - upper) * 2 * B, 2 * B), 2 * B)

    def lanes(place):
        return pl.ds(pl.multiple_of(place * B, B), B)

    def share(step):
        place, device = peer(step)
        return remote(
            pos_ref.at[place], quad.at[own_rows, lanes(mine)], p_send.at[step - 1], p_recv.at[step - 1], device
        )

    for step in (3, 2, 1):
        share(step).start()
    keep = pltpu.make_async_copy(pos_ref.at[mine], quad.at[own_rows, lanes(mine)], keep_sem)
    keep.start()
    for step in (1, 2, 3):
        _, device = peer(step)
        remote(
            pos_ref.at[0], quad.at[own_rows, lanes(sender(step))], p_send.at[step - 1], p_recv.at[step - 1], device
        ).wait_recv()
    keep.wait()

    def cross(part):
        side = upper if part == 0 else 1 - upper
        view = quad.at[own_rows, pl.ds(pl.multiple_of(side * 2 * B, 2 * B), 2 * B)]
        return remote(view, view, y_send.at[part], y_recv.at[part], (far_row, col))

    def crossed(part):
        side = 1 - upper if part == 0 else upper
        view = quad.at[far_rows, pl.ds(pl.multiple_of(side * 2 * B, 2 * B), 2 * B)]
        return remote(view, view, y_send.at[part], y_recv.at[part], (far_row, col))

    cross(0).start()
    cross(1).start()

    row_ids = lax.broadcasted_iota(jnp.int32, (B, B), 0)
    col_ids = lax.broadcasted_iota(jnp.int32, (B, B), 1)

    def reduce_copy(turn, step):
        place, device = peer(step)
        return remote(
            parts.at[turn, place],
            arrived.at[turn, step - 1],
            r_send.at[turn, step - 1],
            r_recv.at[turn, step - 1],
            device,
        )

    def serve_copy(turn, number):
        if number < len(row_targets):
            kind, device = 0, row_targets[number]
        else:
            kind, device = 1, col_targets[number - len(row_targets)]
        return remote(
            gen.at[turn, 0, mine], gen.at[turn, kind, mine], a_send.at[turn, number], a_recv.at[turn, kind], device
        )

    def gather_copy(turn, kind, step):
        _, device = peer(step)
        return remote(
            gen.at[turn, kind, mine],
            gen.at[turn, kind, mine],
            b_send.at[turn, kind, step - 1],
            b_recv.at[turn, kind, step - 1],
            device,
        )

    def gather_wait(turn, kind, step):
        place = sender(step)
        _, device = peer(step)
        remote(
            gen.at[turn, kind, place],
            gen.at[turn, kind, place],
            b_send.at[turn, kind, step - 1],
            b_recv.at[turn, kind, step - 1],
            device,
        ).wait_recv()

    def make_parts(source, turn):
        for pair in (0, 1):
            first, second = block(2 * pair), block(2 * pair + 1)
            head, tail = source[first, first], source[second, second]
            same = row_ids == col_ids
            head_kept, tail_kept = jnp.where(same, head, 0.0), jnp.where(same, tail, 0.0)
            head_across = jnp.sum(head_kept, axis=0, keepdims=True)
            tail_across = jnp.sum(tail_kept, axis=0, keepdims=True)
            head_down = jnp.sum(head_kept, axis=1, keepdims=True)
            tail_down = jnp.sum(tail_kept, axis=1, keepdims=True)
            parts[turn, 2 * pair] = source[second, first] * (head_across - tail_down)
            parts[turn, 2 * pair + 1] = jnp.where(
                row_ids > col_ids, head * (head_across - head_down), tail * (tail_across - tail_down)
            )

    def distribute(source, turn):
        @pl.when(on_diagonal)
        def _():
            if turn == 0:
                crossed(0).wait_recv()
            make_parts(source, turn)
            for step in (3, 2, 1):
                reduce_copy(turn, step).start()
            total = parts[turn, mine]
            for step in (1, 2, 3):
                remote(
                    parts.at[turn, 0],
                    arrived.at[turn, step - 1],
                    r_send.at[turn, step - 1],
                    r_recv.at[turn, step - 1],
                    peer(step)[1],
                ).wait_recv()
                total = total + arrived[turn, step - 1]
            gen[turn, 0, mine] = STEP_SIZE * total
            for step in (3, 2, 1):
                gather_copy(turn, 0, step).start()
            for number in range(len(row_targets) + len(col_targets)):
                serve_copy(turn, number).start()

        @pl.when(off_diagonal)
        def _():
            for kind in (0, 1):
                view = gen.at[turn, kind, mine]
                remote(view, view, b_send.at[turn, kind, 0], a_recv.at[turn, kind], row_source).wait_recv()
                for step in (3, 2, 1):
                    gather_copy(turn, kind, step).start()

        for step in (1, 2, 3):
            gather_wait(turn, 0, step)

    identity = jnp.where(
        lax.broadcasted_iota(jnp.int32, (2 * B, 2 * B), 0) == lax.broadcasted_iota(jnp.int32, (2 * B, 2 * B), 1),
        1.0,
        0.0,
    ).astype(F32)

    def rotation(turn, kind, pair, sign):
        across = gen[turn, kind, 2 * pair] * sign
        mixed = gen[turn, kind, 2 * pair + 1] * sign
        lower = jnp.where(row_ids > col_ids, mixed, 0.0)
        higher = jnp.where(row_ids < col_ids, mixed, 0.0)
        full[:B, :B] = lower - lower.T
        full[B:, B:] = higher - higher.T
        full[B:, :B] = across
        full[:B, B:] = -across.T
        once = full[...]
        halves = split(once)
        twice = product(halves, halves)
        rest = 0.5 * identity + once * (1.0 / 6.0) + twice * (1.0 / 24.0)
        return split(identity + once + product(split(twice), split(rest)))

    def rotations(turn):
        for pair in (0, 1):
            rows_high[pair], rows_low[pair] = rotation(turn, 0, pair, -1.0)

        @pl.when(off_diagonal)
        def _():
            for step in (1, 2, 3):
                gather_wait(turn, 1, step)

        @pl.when(on_diagonal)
        def _():
            gen[turn, 1] = gen[turn, 0]

        for pair in (0, 1):
            cols_high[pair], cols_low[pair] = rotation(turn, 1, pair, 1.0)

    distribute(quad, 0)
    rotations(0)

    @pl.when(off_diagonal)
    def _():
        crossed(0).wait_recv()

    crossed(1).wait_recv()

    for pair in (0, 1):
        moved = product(split(quad[:, pl.ds(pair * 2 * B, 2 * B)]), (cols_high[pair], cols_low[pair]))
        half_done[:, block(pair)] = moved[:, :B]
        half_done[:, block(pair + 2)] = moved[:, B:]
    for pair in (0, 1):
        moved = product((rows_high[pair], rows_low[pair]), split(half_done[pl.ds(pair * 2 * B, 2 * B), :]))
        turned[block(pair), :] = moved[:B]
        turned[block(pair + 2), :] = moved[B:]

    distribute(turned, 1)
    rotations(1)

    def give_back(part, step):
        place, device = peer(step)
        return remote(
            done.at[place, block(part)],
            landed.at[mine, block(part)],
            z_send.at[part, step - 1],
            z_recv.at[part, step - 1],
            device,
        )

    half = pl.ds(pl.multiple_of(upper * B, B), B)
    for part in (0, 1):
        moved = product(
            (rows_high[part, half], rows_low[part, half]), split(turned[pl.ds(part * 2 * B, 2 * B), :])
        )
        for pair in (0, 1):
            final = product(split(moved[:, pair * 2 * B : (pair + 1) * 2 * B]), (cols_high[pair], cols_low[pair]))
            done[pair, block(part)] = final[:, :B]
            done[pair + 2, block(part)] = final[:, B:]
        for step in (3, 2, 1):
            give_back(part, step).start()
    out_ref[mine] = done[mine]
    for part in (0, 1):
        for step in (1, 2, 3):
            place = sender(step)
            remote(
                done.at[0, block(part)],
                landed.at[place, block(part)],
                z_send.at[part, step - 1],
                z_recv.at[part, step - 1],
                peer(step)[1],
            ).wait_recv()
    for step in (1, 2, 3):
        out_ref[sender(step)] = landed[sender(step)]

    for step in (1, 2, 3):
        share(step).wait_send()
    for part in (0, 1):
        cross(part).wait_send()
        for step in (1, 2, 3):
            give_back(part, step).wait_send()
    for turn in (0, 1):
        for step in (1, 2, 3):
            gather_copy(turn, 0, step).wait_send()

        @pl.when(on_diagonal)
        def _():
            for step in (1, 2, 3):
                reduce_copy(turn, step).wait_send()
            for number in range(len(row_targets) + len(col_targets)):
                serve_copy(turn, number).wait_send()

        @pl.when(off_diagonal)
        def _():
            for step in (1, 2, 3):
                gather_copy(turn, 1, step).wait_send()


def local(n_row, n_col, positions):
    dma = pltpu.SemaphoreType.DMA
    n_serve = n_col // 4 - 1 + n_row // 2 - 1
    return pl.pallas_call(
        functools.partial(kernel, n_row, n_col),
        out_shape=jax.ShapeDtypeStruct(positions.shape, F32),
        in_specs=[pl.BlockSpec(memory_space=pltpu.VMEM)],
        out_specs=pl.BlockSpec(memory_space=pltpu.VMEM),
        scratch_shapes=[
            pltpu.VMEM((4 * B, 4 * B), F32),
            pltpu.VMEM((4 * B, 4 * B), F32),
            pltpu.VMEM((4 * B, 4 * B), F32),
            pltpu.VMEM((2, 4, B, B), F32),
            pltpu.VMEM((2, 3, B, B), F32),
            pltpu.VMEM((2, 2, 4, B, B), F32),
            pltpu.VMEM((2 * B, 2 * B), F32),
            pltpu.VMEM((2, 2 * B, 2 * B), BF16),
            pltpu.VMEM((2, 2 * B, 2 * B), BF16),
            pltpu.VMEM((2, 2 * B, 2 * B), BF16),
            pltpu.VMEM((2, 2 * B, 2 * B), BF16),
            pltpu.VMEM((4, 2 * B, B), F32),
            pltpu.VMEM((4, 2 * B, B), F32),
            dma,
            dma((3,)),
            dma((3,)),
            dma((2,)),
            dma((2,)),
            dma((2, 3)),
            dma((2, 3)),
            dma((2, n_serve)),
            dma((2, 2)),
            dma((2, 2, 3)),
            dma((2, 2, 3)),
            dma((2, 3)),
            dma((2, 3)),
        ],
        compiler_params=pltpu.CompilerParams(collective_id=0, has_side_effects=True, vmem_limit_bytes=48 * 2**20),
    )(positions)


def solution(mesh):
    body = functools.partial(local, mesh.shape["row"], mesh.shape["col"])
    spec = P(None, "row", "col")
    return jax.shard_map(body, mesh=mesh, in_specs=(spec,), out_specs=spec, check_vma=False)
```

time: 364 us -> 90.3 us (0.25)
  the two profiles are of different devices: /device:TPU:16 before, /device:TPU:8 now
where the time goes in v1:
time: 90.3 us; the launch traced here: 90.1 us
  Pallas kernels  88.3 us (98%)
  local copies, waits for them, and re-layouts  1.84 us (2%)
    pallas_call x1, Pallas kernels, local(): pl.pallas_call(functools.partial(kernel, n_row, n_col), out_shape=jax.Sha...  88.3 us
    unnamed x3, local copies, waits for them, and re-layouts  1.84 us

profile of v1, /device:TPU:8, one launch (start us, length us, event | category | flops | bytes accessed | tf_op | source)
XLA Modules:
  0.0 90.1 jit_solution(9470645686156049894)
XLA Ops:
  0.0 0.0 copy-start
  0.0 1.0 %copy-done = f32[4,256,128]{2,1,0:T(8,128)S(1)} copy-done((f32[4,256,128]{2,1,0:T(8,128)S(1)}, f32[4,256,128]{2,1,0:T(8,128)}, u32[]{:S(2)}) %copy-start) | copy-done | bytes 524312
  1.0 88.3 %shard_map.17 = f32[4,256,128]{2,1,0:T(8,128)S(1)} custom-call(f32[4,256,128]{2,1,0:T(8,128)S(1)} %copy-done), custom_call_target="tpu_custom_call" | custom-call | tf_op jit(solution)/shard_map/pallas_call | solution.py:367
  89.3 0.8 copy.3
Async XLA Ops:
  0.0 1.0 %copy-start = (f32[4,256,128]{2,1,0:T(8,128)S(1)}, f32[4,256,128]{2,1,0:T(8,128)}, u32[]{:S(2)}) copy-start(f32[4,256,128]{2,1,0:T(8,128)} %pos_ref.1) | copy-start | bytes 1572868

commit v2 on v1

--- a/solution.py
+++ b/solution.py
@@ -32,8 +32,9 @@
 def kernel(
     n_row,
     n_col,
+    source_ref,
+    out_ref,
     pos_ref,
-    out_ref,
     quad,
     half_done,
     turned,
@@ -47,7 +48,20 @@
     cols_low,
     done,
     landed,
+    turn_rows,
+    tri_out,
+    tri_in,
+    centre_out,
+    centre_in,
+    load_sem,
     keep_sem,
+    ready,
+    swap_send,
+    swap_recv,
+    raw_send,
+    raw_recv,
+    piece_send,
+    piece_recv,
     p_send,
     p_recv,
     y_send,
@@ -70,6 +84,10 @@
     mine = 2 * col_high + low
     on_diagonal = row_quad == col_quad
     off_diagonal = row_quad != col_quad
+    owner = jnp.logical_and(on_diagonal, upper == col_high)
+    guest = jnp.logical_and(on_diagonal, upper != col_high)
+    first_owner = jnp.logical_and(owner, low == 0)
+    second_owner = jnp.logical_and(owner, low == 1)
     far_row = lax.rem(row + n_quad, n_row)
 
     def column(quad_id, place):
@@ -88,7 +106,8 @@
         )
 
     reach = REACH[n_row // 4]
-    row_targets = [(row, column(lax.rem(row_quad + hop, n_quad), mine)) for hop in range(1, n_quad)]
+    hops = sorted(range(1, n_quad), key=lambda hop: abs(hop % 4 - 2))
+    row_targets = [(row, column(lax.rem(row_quad + hop, n_quad), mine)) for hop in hops]
     chip, core = lax.div(row, 2), lax.rem(row, 2)
     col_targets = []
     for hop in reach:
@@ -101,20 +120,43 @@
     wraps = lax.div(away + n_row // 8 - (1 if n_row >= 16 else 0), n_row // 4) if n_row >= 16 else lax.div(away, n_row // 4)
     col_source = (lax.rem(col_quad + n_quad * lax.rem(wraps, 2), n_row), col)
 
+    load = pltpu.make_async_copy(source_ref, pos_ref, load_sem)
+    load.start()
+
     barrier = pltpu.get_barrier_semaphore()
+
+    def greet(device):
+        pl.semaphore_signal(barrier, inc=1, device_id=device, device_id_type=MESH)
+
+    @pl.when(on_diagonal)
+    def _():
+        for side in (0, 1):
+            greet((far_row, column(col_quad, 2 * (1 - upper) + side)))
+
     for step in (1, 2, 3):
-        pl.semaphore_signal(barrier, inc=1, device_id=(row, column(col_quad, sender(step))), device_id_type=MESH)
-    pl.semaphore_signal(barrier, inc=1, device_id=(far_row, col), device_id_type=MESH)
+        greet((row, column(col_quad, sender(step))))
 
     @pl.when(off_diagonal)
     def _():
-        pl.semaphore_signal(barrier, inc=1, device_id=row_source, device_id_type=MESH)
-        pl.semaphore_signal(barrier, inc=1, device_id=col_source, device_id_type=MESH)
-        pl.semaphore_wait(barrier, 4)
+        greet((far_row, col))
+        pl.semaphore_wait(barrier, 3 + 1 + 2)
+        for device in (row_source, col_source):
+            pl.semaphore_signal(ready, inc=1, device_id=device, device_id_type=MESH)
 
     @pl.when(on_diagonal)
     def _():
-        pl.semaphore_wait(barrier, 4 + len(row_targets) + len(col_targets))
+        for device in row_targets + col_targets:
+            greet(device)
+
+    @pl.when(owner)
+    def _():
+        pl.semaphore_wait(barrier, 3 + 4)
+
+    @pl.when(guest)
+    def _():
+        pl.semaphore_wait(barrier, 3)
+
+    load.wait()
 
     own_rows = pl.ds(pl.multiple_of(upper * 2 * B, 2 * B), 2 * B)
     far_rows = pl.ds(pl.multiple_of((1 - upper) * 2 * B, 2 * B), 2 * B)
@@ -128,29 +170,14 @@
             pos_ref.at[place], quad.at[own_rows, lanes(mine)], p_send.at[step - 1], p_recv.at[step - 1], device
         )
 
-    for step in (3, 2, 1):
-        share(step).start()
-    keep = pltpu.make_async_copy(pos_ref.at[mine], quad.at[own_rows, lanes(mine)], keep_sem)
-    keep.start()
-    for step in (1, 2, 3):
-        _, device = peer(step)
-        remote(
-            pos_ref.at[0], quad.at[own_rows, lanes(sender(step))], p_send.at[step - 1], p_recv.at[step - 1], device
-        ).wait_recv()
-    keep.wait()
-
-    def cross(part):
-        side = upper if part == 0 else 1 - upper
-        view = quad.at[own_rows, pl.ds(pl.multiple_of(side * 2 * B, 2 * B), 2 * B)]
-        return remote(view, view, y_send.at[part], y_recv.at[part], (far_row, col))
-
-    def crossed(part):
-        side = 1 - upper if part == 0 else upper
-        view = quad.at[far_rows, pl.ds(pl.multiple_of(side * 2 * B, 2 * B), 2 * B)]
-        return remote(view, view, y_send.at[part], y_recv.at[part], (far_row, col))
-
-    cross(0).start()
-    cross(1).start()
+    def raw(place):
+        return remote(
+            pos_ref.at[place],
+            quad.at[own_rows, lanes(mine)],
+            raw_send.at[place],
+            raw_recv.at[low],
+            (far_row, column(col_quad, place)),
+        )
 
     row_ids = lax.broadcasted_iota(jnp.int32, (B, B), 0)
     col_ids = lax.broadcasted_iota(jnp.int32, (B, B), 1)
@@ -194,6 +221,118 @@
             b_recv.at[turn, kind, step - 1],
             device,
         ).wait_recv()
+
+    def centre(tile):
+        kept = jnp.where(row_ids == col_ids, tile, 0.0)
+        return jnp.sum(kept, axis=0, keepdims=True), jnp.sum(kept, axis=1, keepdims=True)
+
+    partner = (row, column(col_quad, mine + 1 - 2 * low))
+    here = gen.at[0, 0, mine]
+    piece = remote(here, here, piece_send, piece_recv, (far_row, col))
+    give_tri = remote(tri_out, tri_in, swap_send, swap_recv, partner)
+    give_centre = remote(centre_out, centre_in, swap_send, swap_recv, partner)
+
+    @pl.when(second_owner)
+    def _():
+        total = jnp.zeros((B, B), F32)
+        for matrix in range(4):
+            tile = pos_ref[matrix, B:]
+            across, down = centre(tile)
+            centre_out[matrix : matrix + 1] = across
+            total = total + tile * (across - down)
+        give_centre.start()
+        tri_out[...] = total
+
+    @pl.when(first_owner)
+    def _():
+        total = jnp.zeros((B, B), F32)
+        for matrix in range(4):
+            tile = pos_ref[matrix, :B]
+            across, down = centre(tile)
+            centre_out[matrix : matrix + 1] = across
+            total = total + tile * (across - down)
+        tri_out[...] = total
+        give_tri.start()
+
+    @pl.when(owner)
+    def _():
+        raw(0).start()
+        raw(1).start()
+
+    for step in (3, 2, 1):
+        share(step).start()
+    keep = pltpu.make_async_copy(pos_ref.at[mine], quad.at[own_rows, lanes(mine)], keep_sem)
+    keep.start()
+
+    @pl.when(second_owner)
+    def _():
+        give_tri.wait_recv()
+        gen[0, 0, mine] = STEP_SIZE * jnp.where(row_ids > col_ids, tri_in[...], tri_out[...])
+
+    @pl.when(first_owner)
+    def _():
+        give_centre.wait_recv()
+        total = jnp.zeros((B, B), F32)
+        for matrix in range(4):
+            _, down = centre(jnp.broadcast_to(centre_in[matrix : matrix + 1], (B, B)))
+            total = total + pos_ref[matrix, B:] * (centre_out[matrix : matrix + 1] - down)
+        gen[0, 0, mine] = STEP_SIZE * total
+
+    @pl.when(owner)
+    def _():
+        piece.start()
+        raw(2).start()
+        raw(3).start()
+
+    def serve(turn):
+        for number in range(len(row_targets) + len(col_targets)):
+            serve_copy(turn, number).start()
+
+    def pass_on(turn):
+        for kind in (0, 1):
+            view = gen.at[turn, kind, mine]
+            remote(view, view, b_send.at[turn, kind, 0], a_recv.at[turn, kind], row_source).wait_recv()
+            for step in (3, 2, 1):
+                gather_copy(turn, kind, step).start()
+
+    @pl.when(guest)
+    def _():
+        piece.wait_recv()
+
+    @pl.when(on_diagonal)
+    def _():
+        for step in (3, 2, 1):
+            gather_copy(0, 0, step).start()
+        pl.semaphore_wait(ready, len(row_targets) + len(col_targets))
+        serve(0)
+
+    own_slab, far_slab = quad.at[own_rows], quad.at[far_rows]
+    cross = remote(own_slab, own_slab, y_send, y_recv, (far_row, col))
+
+    for step in (1, 2, 3):
+        remote(
+            pos_ref.at[0],
+            quad.at[own_rows, lanes(sender(step))],
+            p_send.at[step - 1],
+            p_recv.at[step - 1],
+            peer(step)[1],
+        ).wait_recv()
+    keep.wait()
+
+    @pl.when(off_diagonal)
+    def _():
+        pass_on(0)
+        cross.start()
+
+    def span(side, number):
+        return pl.ds(pl.multiple_of((2 * side + number) * B, B), B)
+
+    @pl.when(on_diagonal)
+    def _():
+        for far in (0, 1):
+            for near in (0, 1):
+                there, back = span(1 - upper, far), span(upper, near)
+                quad[there, back] = quad[back, there].T
 
     def make_parts(source, turn):
         for pair in (0, 1):
@@ -213,8 +352,6 @@
     def distribute(source, turn):
         @pl.when(on_diagonal)
         def _():
-            if turn == 0:
-                crossed(0).wait_recv()
             make_parts(source, turn)
             for step in (3, 2, 1):
                 reduce_copy(turn, step).start()
@@ -231,19 +368,7 @@
             gen[turn, 0, mine] = STEP_SIZE * total
             for step in (3, 2, 1):
                 gather_copy(turn, 0, step).start()
-            for number in range(len(row_targets) + len(col_targets)):
-                serve_copy(turn, number).start()
-
-        @pl.when(off_diagonal)
-        def _():
-            for kind in (0, 1):
-                view = gen.at[turn, kind, mine]
-                remote(view, view, b_send.at[turn, kind, 0], a_recv.at[turn, kind], row_source).wait_recv()
-                for step in (3, 2, 1):
-                    gather_copy(turn, kind, step).start()
-
-        for step in (1, 2, 3):
-            gather_wait(turn, 0, step)
+            serve(turn)
 
     identity = jnp.where(
         lax.broadcasted_iota(jnp.int32, (2 * B, 2 * B), 0) == lax.broadcasted_iota(jnp.int32, (2 * B, 2 * B), 1),
@@ -252,44 +377,58 @@
     ).astype(F32)
 
     def rotation(turn, kind, pair, sign):
+        whole = full.at[pair]
         across = gen[turn, kind, 2 * pair] * sign
         mixed = gen[turn, kind, 2 * pair + 1] * sign
         lower = jnp.where(row_ids > col_ids, mixed, 0.0)
         higher = jnp.where(row_ids < col_ids, mixed, 0.0)
-        full[:B, :B] = lower - lower.T
-        full[B:, B:] = higher - higher.T
-        full[B:, :B] = across
-        full[:B, B:] = -across.T
-        once = full[...]
+        whole[:B, :B] = lower - lower.T
+        whole[B:, B:] = higher - higher.T
+        whole[B:, :B] = across
+        whole[:B, B:] = -across.T
+        once = whole[...]
         halves = split(once)
         twice = product(halves, halves)
         rest = 0.5 * identity + once * (1.0 / 6.0) + twice * (1.0 / 24.0)
-        return split(identity + once + product(split(twice), split(rest)))
+        return identity + once + product(split(twice), split(rest))
 
     def rotations(turn):
+        for step in (1, 2, 3):
+            gather_wait(turn, 0, step)
         for pair in (0, 1):
-            rows_high[pair], rows_low[pair] = rotation(turn, 0, pair, -1.0)
+            turn_rows[pair] = rotation(turn, 0, pair, -1.0)
+        for pair in (0, 1):
+            rows_high[pair], rows_low[pair] = split(turn_rows[pair])
+
+        @pl.when(on_diagonal)
+        def _():
+            for pair in (0, 1):
+                cols_high[pair], cols_low[pair] = split(turn_rows[pair].T)
 
         @pl.when(off_diagonal)
         def _():
             for step in (1, 2, 3):
                 gather_wait(turn, 1, step)
-
-        @pl.when(on_diagonal)
-        def _():
-            gen[turn, 1] = gen[turn, 0]
-
-        for pair in (0, 1):
-            cols_high[pair], cols_low[pair] = rotation(turn, 1, pair, 1.0)
-
-    distribute(quad, 0)
+            for pair in (0, 1):
+                cols_high[pair], cols_low[pair] = split(rotation(turn, 1, pair, 1.0))
+
     rotations(0)
 
+    @pl.when(on_diagonal)
+    def _():
+        for side in (0, 1):
+            remote(
+                pos_ref.at[0],
+                quad.at[far_rows, lanes(2 * (1 - upper) + side)],
+                raw_send.at[side],
+                raw_recv.at[side],
+                (far_row, col),
+            ).wait_recv()
+
     @pl.when(off_diagonal)
     def _():
-        crossed(0).wait_recv()
-
-    crossed(1).wait_recv()
+        pass_on(1)
+        remote(far_slab, far_slab, y_send, y_recv, (far_row, col)).wait_recv()
 
     for pair in (0, 1):
         moved = product(split(quad[:, pl.ds(pair * 2 * B, 2 * B)]), (cols_high[pair], cols_low[pair]))
@@ -341,7 +480,6 @@
     for step in (1, 2, 3):
         share(step).wait_send()
     for part in (0, 1):
-        cross(part).wait_send()
         for step in (1, 2, 3):
             give_back(part, step).wait_send()
     for turn in (0, 1):
@@ -350,8 +488,9 @@
 
         @pl.when(on_diagonal)
         def _():
-            for step in (1, 2, 3):
-                reduce_copy(turn, step).wait_send()
+            if turn == 1:
+                for step in (1, 2, 3):
+                    reduce_copy(turn, step).wait_send()
             for number in range(len(row_targets) + len(col_targets)):
                 serve_copy(turn, number).wait_send()
 
@@ -359,6 +498,22 @@
         def _():
             for step in (1, 2, 3):
                 gather_copy(turn, 1, step).wait_send()
+            if turn == 0:
+                cross.wait_send()
+
+    @pl.when(first_owner)
+    def _():
+        give_tri.wait_send()
+
+    @pl.when(second_owner)
+    def _():
+        give_centre.wait_send()
+
+    @pl.when(owner)
+    def _():
+        piece.wait_send()
+        for place in range(4):
+            raw(place).wait_send()
 
 
 def local(n_row, n_col, positions):
@@ -367,27 +522,41 @@
     return pl.pallas_call(
         functools.partial(kernel, n_row, n_col),
         out_shape=jax.ShapeDtypeStruct(positions.shape, F32),
-        in_specs=[pl.BlockSpec(memory_space=pltpu.VMEM)],
+        in_specs=[pl.BlockSpec(memory_space=pltpu.HBM)],
         out_specs=pl.BlockSpec(memory_space=pltpu.VMEM),
         scratch_shapes=[
+            pltpu.VMEM((4, 2 * B, B), F32),
             pltpu.VMEM((4 * B, 4 * B), F32),
             pltpu.VMEM((4 * B, 4 * B), F32),
             pltpu.VMEM((4 * B, 4 * B), F32),
             pltpu.VMEM((2, 4, B, B), F32),
             pltpu.VMEM((2, 3, B, B), F32),
             pltpu.VMEM((2, 2, 4, B, B), F32),
-            pltpu.VMEM((2 * B, 2 * B), F32),
+            pltpu.VMEM((2, 2 * B, 2 * B), F32),
             pltpu.VMEM((2, 2 * B, 2 * B), BF16),
             pltpu.VMEM((2, 2 * B, 2 * B), BF16),
             pltpu.VMEM((2, 2 * B, 2 * B), BF16),
             pltpu.VMEM((2, 2 * B, 2 * B), BF16),
             pltpu.VMEM((4, 2 * B, B), F32),
             pltpu.VMEM((4, 2 * B, B), F32),
+            pltpu.VMEM((2, 2 * B, 2 * B), F32),
+            pltpu.VMEM((B, B), F32),
+            pltpu.VMEM((B, B), F32),
+            pltpu.VMEM((8, B), F32),
+            pltpu.VMEM((8, B), F32),
+            dma,
+            dma,
+            pltpu.SemaphoreType.REGULAR,
+            dma,
+            dma,
+            dma((4,)),
+            dma((2,)),
+            dma,
             dma,
             dma((3,)),
             dma((3,)),
-            dma((2,)),
-            dma((2,)),
+            dma,
+            dma,
             dma((2, 3)),
             dma((2, 3)),
             dma((2, n_serve)),

time: 90.3 us -> 74.5 us (0.83)
  the two profiles are of different devices: /device:TPU:8 before, /device:TPU:24 now
where the time goes in v2:
time: 74.5 us; the launch traced here: 74.4 us
  Pallas kernels  72.5 us (97%)
  local copies, waits for them, and re-layouts  1.84 us (2%)
    pallas_call x1, Pallas kernels, local(): pl.pallas_call(functools.partial(kernel, n_row, n_col), out_shape=jax.Sha...  72.5 us
    unnamed x3, local copies, waits for them, and re-layouts  1.84 us

profile of v2, /device:TPU:24, one launch (start us, length us, event | category | flops | bytes accessed | tf_op | source)
XLA Modules:
  0.0 74.4 jit_solution(11216650199468932025)
XLA Ops:
  0.0 0.0 copy-start
  0.0 1.0 %copy-done = f32[4,256,128]{2,1,0:T(8,128)S(1)} copy-done((f32[4,256,128]{2,1,0:T(8,128)S(1)}, f32[4,256,128]{2,1,0:T(8,128)}, u32[]{:S(2)}) %copy-start) | copy-done | bytes 524312
  1.0 72.5 %shard_map.17 = f32[4,256,128]{2,1,0:T(8,128)S(1)} custom-call(f32[4,256,128]{2,1,0:T(8,128)S(1)} %copy-done), custom_call_target="tpu_custom_call" | custom-call | tf_op jit(solution)/shard_map/pallas_call | solution.py:522
  73.6 0.8 %copy.3 = f32[4,256,128]{2,1,0:T(8,128)} copy(f32[4,256,128]{2,1,0:T(8,128)S(1)} %shard_map.17) | data formatting | bytes 1048576
Async XLA Ops:
  0.0 1.0 %copy-start = (f32[4,256,128]{2,1,0:T(8,128)S(1)}, f32[4,256,128]{2,1,0:T(8,128)}, u32[]{:S(2)}) copy-start(f32[4,256,128]{2,1,0:T(8,128)} %source_ref.1) | copy-start | bytes 1572868

commit v3 on v2

--- a/solution.py
+++ b/solution.py
@@ -62,6 +62,8 @@
     raw_recv,
     piece_send,
     piece_recv,
+    f_send,
+    f_recv,
     p_send,
     p_recv,
     y_send,
@@ -88,17 +90,21 @@
     guest = jnp.logical_and(on_diagonal, upper != col_high)
     first_owner = jnp.logical_and(owner, low == 0)
     second_owner = jnp.logical_and(owner, low == 1)
+    core = lax.rem(row, 2)
+    sibling = (row + 1 - 2 * core, col)
+    leader = jnp.logical_and(off_diagonal, core == lax.rem(col_quad, 2))
+    follower = core != lax.rem(col_quad, 2)
     far_row = lax.rem(row + n_quad, n_row)
 
     def column(quad_id, place):
         return (n_col // 2) * lax.div(place, 2) + 2 * quad_id + lax.rem(place, 2)
 
     def peer(step):
-        place = lax.rem(mine + step, 4)
+        place = 2 * (1 - col_high if step >= 2 else col_high) + (1 - low if step % 2 else low)
         return place, (row, column(col_quad, place))
 
     def sender(step):
-        return lax.rem(mine + 4 - step, 4)
+        return peer(step)[0]
 
     def remote(src, dst, send, recv, device):
         return pltpu.make_async_remote_copy(
@@ -108,17 +114,21 @@
     reach = REACH[n_row // 4]
     hops = sorted(range(1, n_quad), key=lambda hop: abs(hop % 4 - 2))
     row_targets = [(row, column(lax.rem(row_quad + hop, n_quad), mine)) for hop in hops]
-    chip, core = lax.div(row, 2), lax.rem(row, 2)
-    col_targets = []
-    for hop in reach:
-        there = lax.rem(chip + n_row // 2 + hop, n_row // 2)
-        col_targets.append((2 * there + 1 - core, col))
-        if hop != 0:
-            col_targets.append((2 * there + core, col))
+    chip = lax.div(row, 2)
+    n_chip = n_row // 2
+
+    def above(hop):
+        return 2 * lax.rem(chip + n_chip + hop, n_chip) + core, col
+
+    col_targets = [above(hop) for hop in reach if hop != 0]
+    other_targets = [above(n_chip // 2 + hop) for hop in reach if hop != 0]
     row_source = (row, column(row_quad, mine))
     away = lax.rem(chip + n_row // 2 - lax.div(col_quad, 2), n_row // 2)
     wraps = lax.div(away + n_row // 8 - (1 if n_row >= 16 else 0), n_row // 4) if n_row >= 16 else lax.div(away, n_row // 4)
     col_source = (lax.rem(col_quad + n_quad * lax.rem(wraps, 2), n_row), col)
+    col_owner = (col_quad + n_quad * col_high, col)
+    near_owner = jnp.logical_and(leader, lax.rem(wraps, 2) == col_high)
+    far_owner = jnp.logical_and(leader, lax.rem(wraps, 2) != col_high)
 
     load = pltpu.make_async_copy(source_ref, pos_ref, load_sem)
     load.start()
@@ -139,9 +149,10 @@
     @pl.when(off_diagonal)
     def _():
         greet((far_row, col))
-        pl.semaphore_wait(barrier, 3 + 1 + 2)
-        for device in (row_source, col_source):
-            pl.semaphore_signal(ready, inc=1, device_id=device, device_id_type=MESH)
+
+    @pl.when(follower)
+    def _():
+        greet(sibling)
 
     @pl.when(on_diagonal)
     def _():
@@ -150,11 +161,37 @@
 
     @pl.when(owner)
     def _():
-        pl.semaphore_wait(barrier, 3 + 4)
+        for device in other_targets:
+            greet(device)
+
+    def answer(device):
+        pl.semaphore_signal(ready, inc=1, device_id=device, device_id_type=MESH)
+
+    @pl.when(follower)
+    def _():
+        pl.semaphore_wait(barrier, 3 + 1 + 1)
+        answer(row_source)
+
+    @pl.when(near_owner)
+    def _():
+        pl.semaphore_wait(barrier, 3 + 1 + 2 + 1)
+        answer(row_source)
+        answer(col_source)
+
+    @pl.when(far_owner)
+    def _():
+        pl.semaphore_wait(barrier, 3 + 1 + 3 + 1)
+        answer(row_source)
+        answer(col_source)
+        answer(col_owner)
+
+    @pl.when(owner)
+    def _():
+        pl.semaphore_wait(barrier, 3 + 4 + 1)
 
     @pl.when(guest)
     def _():
-        pl.semaphore_wait(barrier, 3)
+        pl.semaphore_wait(barrier, 3 + 1)
 
     load.wait()
 
@@ -192,13 +229,11 @@
             device,
         )
 
-    def serve_copy(turn, number):
-        if number < len(row_targets):
-            kind, device = 0, row_targets[number]
-        else:
-            kind, device = 1, col_targets[number - len(row_targets)]
+    def serve_copy(turn, kind, number):
+        device = (row_targets if kind == 0 else col_targets + other_targets)[number]
+        slot = number + kind * len(row_targets)
         return remote(
-            gen.at[turn, 0, mine], gen.at[turn, kind, mine], a_send.at[turn, number], a_recv.at[turn, kind], device
+            gen.at[turn, 0, mine], gen.at[turn, kind, mine], a_send.at[turn, slot], a_recv.at[turn, kind], device
         )
 
     def gather_copy(turn, kind, step):
@@ -256,8 +291,8 @@
 
     @pl.when(owner)
     def _():
-        raw(0).start()
-        raw(1).start()
+        for place in range(4):
+            raw(place).start()
 
     for step in (3, 2, 1):
         share(step).start()
@@ -281,19 +316,31 @@
     @pl.when(owner)
     def _():
         piece.start()
-        raw(2).start()
-        raw(3).start()
-
-    def serve(turn):
-        for number in range(len(row_targets) + len(col_targets)):
-            serve_copy(turn, number).start()
-
-    def pass_on(turn):
-        for kind in (0, 1):
-            view = gen.at[turn, kind, mine]
-            remote(view, view, b_send.at[turn, kind, 0], a_recv.at[turn, kind], row_source).wait_recv()
-            for step in (3, 2, 1):
-                gather_copy(turn, kind, step).start()
+        pl.semaphore_wait(ready, len(row_targets) + len(col_targets) + len(other_targets))
+        for number in reversed(range(len(col_targets) + len(other_targets))):
+            serve_copy(0, 1, number).start()
+
+    def serve_rows(turn):
+        for number in range(len(row_targets)):
+            serve_copy(turn, 0, number).start()
+
+    def arrive(turn, kind):
+        view = gen.at[turn, kind, mine]
+        remote(view, view, b_send.at[turn, kind, 0], a_recv.at[turn, kind], row_source).wait_recv()
+        for step in (3, 2, 1):
+            gather_copy(turn, kind, step).start()
+
+    def hand(turn, step, kind):
+        place = mine if step == 0 else sender(step)
+        return remote(
+            gen.at[turn, kind, place], gen.at[turn, 1, place], f_send.at[turn, step], f_recv.at[turn, step], sibling
+        )
+
+    def pass_on_column(turn):
+        @pl.when(leader)
+        def _():
+            arrive(turn, 1)
+            hand(turn, 0, 1).start()
 
     @pl.when(guest)
     def _():
@@ -303,26 +350,51 @@
     def _():
         for step in (3, 2, 1):
             gather_copy(0, 0, step).start()
+
+    @pl.when(guest)
+    def _():
         pl.semaphore_wait(ready, len(row_targets) + len(col_targets))
-        serve(0)
-
-    own_slab, far_slab = quad.at[own_rows], quad.at[far_rows]
-    cross = remote(own_slab, own_slab, y_send, y_recv, (far_row, col))
-
-    for step in (1, 2, 3):
-        remote(
-            pos_ref.at[0],
-            quad.at[own_rows, lanes(sender(step))],
-            p_send.at[step - 1],
-            p_recv.at[step - 1],
-            peer(step)[1],
-        ).wait_recv()
+
+    @pl.when(on_diagonal)
+    def _():
+        serve_rows(0)
+
+    def cross(step):
+        place = mine if step == 0 else sender(step)
+        view = quad.at[own_rows, lanes(place)]
+        return remote(pos_ref.at[mine] if step == 0 else view, view, y_send.at[step], y_recv.at[step], (far_row, col))
+
+    def crossed(step):
+        view = quad.at[far_rows, lanes(mine if step == 0 else sender(step))]
+        return remote(view, view, y_send.at[step], y_recv.at[step], (far_row, col))
+
+    def shared(step):
+        view = quad.at[own_rows, lanes(sender(step))]
+        return remote(pos_ref.at[0], view, p_send.at[step - 1], p_recv.at[step - 1], peer(step)[1])
+
+    @pl.when(off_diagonal)
+    def _():
+        for step in (1, 2, 3):
+            shared(step).wait_recv()
+
+    @pl.when(on_diagonal)
+    def _():
+        for step in (1, 2, 3):
+            shared(step).wait_recv()
+
     keep.wait()
 
+    pass_on_column(0)
+
+    @pl.when(follower)
+    def _():
+        hand(0, 0, 1).wait_recv()
+
     @pl.when(off_diagonal)
     def _():
-        pass_on(0)
-        cross.start()
+        for step in range(4):
+            cross(step).start()
+        arrive(0, 0)
 
     def span(side, number):
         return pl.ds(pl.multiple_of((2 * side + number) * B, B), B)
@@ -368,7 +440,9 @@
             gen[turn, 0, mine] = STEP_SIZE * total
             for step in (3, 2, 1):
                 gather_copy(turn, 0, step).start()
-            serve(turn)
+            for number in range(len(col_targets)):
+                serve_copy(turn, 1, number).start()
+            serve_rows(turn)
 
     identity = jnp.where(
         lax.broadcasted_iota(jnp.int32, (2 * B, 2 * B), 0) == lax.broadcasted_iota(jnp.int32, (2 * B, 2 * B), 1),
@@ -395,6 +469,18 @@
     def rotations(turn):
         for step in (1, 2, 3):
             gather_wait(turn, 0, step)
+
+        @pl.when(on_diagonal)
+        def _():
+            for step in range(4):
+                hand(turn, step, 0).start()
+
+        @pl.when(leader)
+        def _():
+            for step in (1, 2, 3):
+                gather_wait(turn, 1, step)
+                hand(turn, step, 1).start()
+
         for pair in (0, 1):
             turn_rows[pair] = rotation(turn, 0, pair, -1.0)
         for pair in (0, 1):
@@ -405,10 +491,13 @@
             for pair in (0, 1):
                 cols_high[pair], cols_low[pair] = split(turn_rows[pair].T)
 
+        @pl.when(follower)
+        def _():
+            for step in range(1 if turn == 0 else 0, 4):
+                hand(turn, step, 1).wait_recv()
+
         @pl.when(off_diagonal)
         def _():
-            for step in (1, 2, 3):
-                gather_wait(turn, 1, step)
             for pair in (0, 1):
                 cols_high[pair], cols_low[pair] = split(rotation(turn, 1, pair, 1.0))
 
@@ -427,8 +516,14 @@
 
     @pl.when(off_diagonal)
     def _():
-        pass_on(1)
-        remote(far_slab, far_slab, y_send, y_recv, (far_row, col)).wait_recv()
+        arrive(1, 0)
+
+    pass_on_column(1)
+
+    @pl.when(off_diagonal)
+    def _():
+        for step in range(4):
+            crossed(step).wait_recv()
 
     for pair in (0, 1):
         moved = product(split(quad[:, pl.ds(pair * 2 * B, 2 * B)]), (cols_high[pair], cols_low[pair]))
@@ -491,15 +586,26 @@
             if turn == 1:
                 for step in (1, 2, 3):
                     reduce_copy(turn, step).wait_send()
-            for number in range(len(row_targets) + len(col_targets)):
-                serve_copy(turn, number).wait_send()
-
-        @pl.when(off_diagonal)
+                for number in range(len(col_targets)):
+                    serve_copy(turn, 1, number).wait_send()
+            for number in range(len(row_targets)):
+                serve_copy(turn, 0, number).wait_send()
+
+            for step in range(4):
+                hand(turn, step, 0).wait_send()
+
+        @pl.when(leader)
         def _():
             for step in (1, 2, 3):
                 gather_copy(turn, 1, step).wait_send()
+            for step in range(4):
+                hand(turn, step, 1).wait_send()
+
+        @pl.when(off_diagonal)
+        def _():
             if turn == 0:
-                cross.wait_send()
+                for step in range(4):
+                    cross(step).wait_send()
 
     @pl.when(first_owner)
     def _():
@@ -512,13 +618,15 @@
     @pl.when(owner)
     def _():
         piece.wait_send()
+        for number in range(len(col_targets) + len(other_targets)):
+            serve_copy(0, 1, number).wait_send()
         for place in range(4):
             raw(place).wait_send()
 
 
 def local(n_row, n_col, positions):
     dma = pltpu.SemaphoreType.DMA
-    n_serve = n_col // 4 - 1 + n_row // 2 - 1
+    n_serve = n_col // 4 - 1 + 2 * (n_row // 4 - 1)
     return pl.pallas_call(
         functools.partial(kernel, n_row, n_col),
         out_shape=jax.ShapeDtypeStruct(positions.shape, F32),
@@ -553,10 +661,12 @@
             dma((2,)),
             dma,
             dma,
+            dma((2, 4)),
+            dma((2, 4)),
             dma((3,)),
             dma((3,)),
-            dma,
-            dma,
+            dma((4,)),
+            dma((4,)),
             dma((2, 3)),
             dma((2, 3)),
             dma((2, n_serve)),

time: 74.5 us -> 67.7 us (0.909)
  the two profiles are of different devices: /device:TPU:24 before, /device:TPU:480 now
where the time goes in v3:
time: 67.7 us; the launch traced here: 67.5 us
  Pallas kernels  65.7 us (97%)
  local copies, waits for them, and re-layouts  1.84 us (3%)
    pallas_call x1, Pallas kernels, local(): pl.pallas_call(functools.partial(kernel, n_row, n_col), out_shape=jax.Sha...  65.7 us
    unnamed x3, local copies, waits for them, and re-layouts  1.84 us

profile of v3, /device:TPU:480, one launch (start us, length us, event | category | flops | bytes accessed | tf_op | source)
XLA Modules:
  0.0 67.5 jit_solution(9300716346847984862)
XLA Ops:
  0.0 0.0 copy-start
  0.0 1.0 %copy-done = f32[4,256,128]{2,1,0:T(8,128)S(1)} copy-done((f32[4,256,128]{2,1,0:T(8,128)S(1)}, f32[4,256,128]{2,1,0:T(8,128)}, u32[]{:S(2)}) %copy-start) | copy-done | bytes 524312
  1.0 65.7 %shard_map.17 = f32[4,256,128]{2,1,0:T(8,128)S(1)} custom-call(f32[4,256,128]{2,1,0:T(8,128)S(1)} %copy-done), custom_call_target="tpu_custom_call" | custom-call | tf_op jit(solution)/shard_map/pallas_call | solution.py:630
  66.7 0.8 %copy.3 = f32[4,256,128]{2,1,0:T(8,128)} copy(f32[4,256,128]{2,1,0:T(8,128)S(1)} %shard_map.17) | data formatting | bytes 1048576
Async XLA Ops:
  0.0 1.0 %copy-start = (f32[4,256,128]{2,1,0:T(8,128)S(1)}, f32[4,256,128]{2,1,0:T(8,128)}, u32[]{:S(2)}) copy-start(f32[4,256,128]{2,1,0:T(8,128)} %source_ref.1) | copy-start | bytes 1572868

commit v4 on v3

--- a/solution.py
+++ b/solution.py
@@ -122,6 +122,8 @@
 
     col_targets = [above(hop) for hop in reach if hop != 0]
     other_targets = [above(n_chip // 2 + hop) for hop in reach if hop != 0]
+    col_hops = [hop % n_chip for hop in reach if hop != 0] + [(n_chip // 2 + hop) % n_chip for hop in reach if hop != 0]
+    far_first = sorted(range(len(col_hops)), key=lambda number: -min(col_hops[number], n_chip - col_hops[number]))
     row_source = (row, column(row_quad, mine))
     away = lax.rem(chip + n_row // 2 - lax.div(col_quad, 2), n_row // 2)
     wraps = lax.div(away + n_row // 8 - (1 if n_row >= 16 else 0), n_row // 4) if n_row >= 16 else lax.div(away, n_row // 4)
@@ -291,7 +293,7 @@
 
     @pl.when(owner)
     def _():
-        for place in range(4):
+        for place in range(3):
             raw(place).start()
 
     for step in (3, 2, 1):
@@ -316,8 +318,9 @@
     @pl.when(owner)
     def _():
         piece.start()
+        raw(3).start()
         pl.semaphore_wait(ready, len(row_targets) + len(col_targets) + len(other_targets))
-        for number in reversed(range(len(col_targets) + len(other_targets))):
+        for number in far_first:
             serve_copy(0, 1, number).start()
 
     def serve_rows(turn):
@@ -359,6 +362,15 @@
     def _():
         serve_rows(0)
 
+    @pl.when(owner)
+    def _():
+        for number in far_first:
+            serve_copy(0, 1, number).wait_send()
+
+    @pl.when(on_diagonal)
+    def _():
+        hand(0, 0, 0).start()
+
     def cross(step):
         place = mine if step == 0 else sender(step)
         view = quad.at[own_rows, lanes(place)]
@@ -392,9 +404,12 @@
 
     @pl.when(off_diagonal)
     def _():
-        for step in range(4):
+        for step in range(2):
             cross(step).start()
         arrive(0, 0)
+        for step in range(2, 4):
+            crossed(step - 2).wait_recv()
+            cross(step).start()
 
     def span(side, number):
         return pl.ds(pl.multiple_of((2 * side + number) * B, B), B)
@@ -438,11 +453,11 @@
                 ).wait_recv()
                 total = total + arrived[turn, step - 1]
             gen[turn, 0, mine] = STEP_SIZE * total
-            for step in (3, 2, 1):
-                gather_copy(turn, 0, step).start()
             for number in range(len(col_targets)):
                 serve_copy(turn, 1, number).start()
             serve_rows(turn)
+            for step in (3, 2, 1):
+                gather_copy(turn, 0, step).start()
 
     identity = jnp.where(
         lax.broadcasted_iota(jnp.int32, (2 * B, 2 * B), 0) == lax.broadcasted_iota(jnp.int32, (2 * B, 2 * B), 1),
@@ -472,7 +487,7 @@
 
         @pl.when(on_diagonal)
         def _():
-            for step in range(4):
+            for step in range(1 if turn == 0 else 0, 4):
                 hand(turn, step, 0).start()
 
         @pl.when(leader)
@@ -522,7 +537,7 @@
 
     @pl.when(off_diagonal)
     def _():
-        for step in range(4):
+        for step in range(2, 4):
             crossed(step).wait_recv()
 
     for pair in (0, 1):
@@ -618,8 +633,6 @@
     @pl.when(owner)
     def _():
         piece.wait_send()
-        for number in range(len(col_targets) + len(other_targets)):
-            serve_copy(0, 1, number).wait_send()
         for place in range(4):
             raw(place).wait_send()
 
@@ -677,7 +690,7 @@
             dma((2, 3)),
         ],
         compiler_params=pltpu.CompilerParams(collective_id=0, has_side_effects=True, vmem_limit_bytes=48 * 2**20),
-    )(positions)
+    )(pltpu.with_memory_space_constraint(positions, pltpu.HBM))
 
 
 def solution(mesh):

time: 67.7 us -> 66.4 us (0.981)
  the two profiles are of different devices: /device:TPU:480 before, /device:TPU:465 now
where the time goes in v4:
time: 66.4 us; the launch traced here: 66.3 us
  Pallas kernels  65.5 us (99%)
  local copies, waits for them, and re-layouts  0.8 us (1%)
    pallas_call x1, Pallas kernels, local(): pl.pallas_call(functools.partial(kernel, n_row, n_col), out_shape=jax.Sha...  65.5 us

profile of v4, /device:TPU:465, one launch (start us, length us, event | category | flops | bytes accessed | tf_op | source)
XLA Modules:
  0.0 66.3 jit_solution(16355610813840641447)
XLA Ops:
  0.0 65.5 %shard_map.17 = f32[4,256,128]{2,1,0:T(8,128)S(1)} custom-call(f32[4,256,128]{2,1,0:T(8,128)} %source_ref.1), custom_call_target="tpu_custom_call" | custom-call | tf_op jit(solution)/shard_map/pallas_call | solution.py:643
  65.5 0.8 %copy.3 = f32[4,256,128]{2,1,0:T(8,128)} copy(f32[4,256,128]{2,1,0:T(8,128)S(1)} %shard_map.17) | data formatting | bytes 1048576

commit v5 on v4

--- a/solution.py
+++ b/solution.py
@@ -481,7 +481,7 @@
         rest = 0.5 * identity + once * (1.0 / 6.0) + twice * (1.0 / 24.0)
         return identity + once + product(split(twice), split(rest))
 
-    def rotations(turn):
+    def rotations(turn, between):
         for step in (1, 2, 3):
             gather_wait(turn, 0, step)
 
@@ -506,6 +506,8 @@
             for pair in (0, 1):
                 cols_high[pair], cols_low[pair] = split(turn_rows[pair].T)
 
+        between()
+
         @pl.when(follower)
         def _():
             for step in range(1 if turn == 0 else 0, 4):
@@ -516,7 +518,7 @@
             for pair in (0, 1):
                 cols_high[pair], cols_low[pair] = split(rotation(turn, 1, pair, 1.0))
 
-    rotations(0)
+    rotations(0, lambda: None)
 
     @pl.when(on_diagonal)
     def _():
@@ -550,7 +552,15 @@
         turned[block(pair + 2), :] = moved[B:]
 
     distribute(turned, 1)
-    rotations(1)
+    half = pl.ds(pl.multiple_of(upper * B, B), B)
+
+    def left_products():
+        for part in (0, 1):
+            half_done[block(part), :] = product(
+                (rows_high[part, half], rows_low[part, half]), split(turned[pl.ds(part * 2 * B, 2 * B), :])
+            )
+
+    rotations(1, left_products)
 
     def give_back(part, step):
         place, device = peer(step)
@@ -562,13 +572,10 @@
             device,
         )
 
-    half = pl.ds(pl.multiple_of(upper * B, B), B)
     for part in (0, 1):
-        moved = product(
-            (rows_high[part, half], rows_low[part, half]), split(turned[pl.ds(part * 2 * B, 2 * B), :])
-        )
         for pair in (0, 1):
-            final = product(split(moved[:, pair * 2 * B : (pair + 1) * 2 * B]), (cols_high[pair], cols_low[pair]))
+            moved = half_done[block(part), pl.ds(pair * 2 * B, 2 * B)]
+            final = product(split(moved), (cols_high[pair], cols_low[pair]))
             done[pair, block(part)] = final[:, :B]
             done[pair + 2, block(part)] = final[:, B:]
         for step in (3, 2, 1):
@@ -584,8 +591,7 @@
                 z_recv.at[part, step - 1],
                 peer(step)[1],
             ).wait_recv()
-    for step in (1, 2, 3):
-        out_ref[sender(step)] = landed[sender(step)]
+            out_ref[place, block(part)] = landed[place, block(part)]
 
     for step in (1, 2, 3):
         share(step).wait_send()

time: 66.4 us -> 66.6 us (level)
  no operation moved by 1% of the time
where the time goes in v5:
time: 66.6 us; the launch traced here: 66.5 us
  Pallas kernels  65.7 us (99%)
  local copies, waits for them, and re-layouts  0.8 us (1%)
    pallas_call x1, Pallas kernels, local(): pl.pallas_call(functools.partial(kernel, n_row, n_col), out_shape=jax.Sha...  65.7 us

profile of v5, /device:TPU:465, one launch (start us, length us, event | category | flops | bytes accessed | tf_op | source)
XLA Modules:
  0.0 66.5 jit_solution(4023262463198440552)
XLA Ops:
  0.0 65.7 %shard_map.17 = f32[4,256,128]{2,1,0:T(8,128)S(1)} custom-call(f32[4,256,128]{2,1,0:T(8,128)} %source_ref.1), custom_call_target="tpu_custom_call" | custom-call | tf_op jit(solution)/shard_map/pallas_call | solution.py:649
  65.7 0.8 %copy.3 = f32[4,256,128]{2,1,0:T(8,128)} copy(f32[4,256,128]{2,1,0:T(8,128)S(1)} %shard_map.17) | data formatting | bytes 1048576
